TPU v7x, 512 devices: a whole 4x8x8 slice. The times are simulated.
512 devices in a mesh: req: 32 (over y_hi, x, core), tp: 16 (over z, y_lo).
Axes of the slice: x: 4, y: 8 (y_hi: 4, y_lo: 2; y = y_hi * 2 + y_lo), z: 8, core: 2. Of those that a mesh axis runs over, the one named last changes fastest.
Arguments:
- hidden: bfloat16 [32, 256, 4096], P('req', None, 'tp'), may hold values from -6 to 6
- norm_gain: bfloat16 [4096], P('tp'), may hold values from 0.5 to 1.5
- w_query: bfloat16 [4096, 2048], P(None, 'tp'), may hold values from -0.09375 to 0.09375
- w_key: bfloat16 [4096, 2048], P(None, 'tp'), may hold values from -0.09375 to 0.09375
- w_value: bfloat16 [4096, 2048], P(None, 'tp'), may hold values from -0.09375 to 0.09375
- w_out: bfloat16 [2048, 4096], P('tp'), may hold values from -0.5 to 0.5
- prefix_keys: bfloat16 [16384, 2048], P('req', 'tp'), may hold values from -1000 to 1000
- prefix_values: bfloat16 [16384, 2048], P('req', 'tp'), may hold values from -6 to 6
- lengths: int32 [32], P('req'), may hold values from 32 to 256, as said below
Outputs:
- attended: bfloat16 [32, 256, 4096], P('req', 'tp')
Inputs may be any that keep to these rules, and one draw needn't show every extreme that they name: `lengths`: every request has at least 32 suffix tokens; in every draw some request has exactly 256.
All inputs are finite; a program needn't handle non-finite values.
Results may differ from a plain program's by a relative error of at most 0.029.
Values may be sent and summed in bfloat16 or wider, within the bound.
A program may use at most 64 MiB of HBM per device.

v0:
```python
import jax
import jax.numpy as jnp
from jax import lax
from jax.sharding import PartitionSpec as P


def rotate(values, angles):
    half = values.shape[-1] // 2
    cosine = jnp.cos(angles)
    sine = jnp.sin(angles)
    first = values[..., :half]
    second = values[..., half:]
    return jnp.concatenate(
        [first * cosine - second * sine, second * cosine + first * sine], axis=-1
    )


def on_device(
    hidden, norm_gain, w_query, w_key, w_value, w_out, prefix_keys, prefix_values, lengths
):
    full, gain = (
        lax.all_gather(hidden, "tp", axis=2, tiled=True),
        lax.all_gather(norm_gain, "tp", axis=0, tiled=True),
    )
    x = full[0].astype(jnp.float32)
    slot = x.shape[0]
    head_dim = w_query.shape[1]
    groups = lax.axis_size("req")
    prefix = prefix_keys.shape[0] * groups
    normed = (
        x * lax.rsqrt(jnp.mean(x * x, axis=-1, keepdims=True) + 1e-05) * gain.astype(jnp.float32)
    ).astype(jnp.bfloat16)
    positions = (prefix + jnp.arange(slot)).astype(jnp.float32)
    freq = 10000.0 ** (-2.0 * jnp.arange(head_dim // 2).astype(jnp.float32) / head_dim)
    angles = positions[:, None] * freq[None, :]
    query = rotate(jnp.dot(normed, w_query, preferred_element_type=jnp.float32), angles).astype(
        jnp.bfloat16
    )
    key_new = rotate(jnp.dot(normed, w_key, preferred_element_type=jnp.float32), angles).astype(
        jnp.bfloat16
    )
    value_new = jnp.dot(normed, w_value, preferred_element_type=jnp.float32).astype(jnp.bfloat16)
    scale = 1.0 / head_dim**0.5
    causal = jnp.arange(slot)[:, None] >= jnp.arange(slot)[None, :]
    own_scores = jnp.einsum("sd,td->st", query, key_new, preferred_element_type=jnp.float32) * scale
    own_scores = jnp.where(causal, own_scores, -jnp.inf)
    top = jnp.max(own_scores, axis=-1)
    own_weights = jnp.where(causal, jnp.exp(own_scores - top[:, None]), 0.0).astype(jnp.bfloat16)
    total = jnp.sum(own_weights.astype(jnp.float32), axis=-1)
    acc = jnp.dot(own_weights, value_new, preferred_element_type=jnp.float32)
    run_total = total
    run_acc = acc
    keys = lax.all_gather(prefix_keys, "req", axis=0, tiled=True)
    values = lax.all_gather(prefix_values, "req", axis=0, tiled=True)
    scores = jnp.einsum("sd,pd->sp", query, keys, preferred_element_type=jnp.float32) * scale
    new_top = jnp.maximum(top, jnp.max(scores, axis=-1))
    fade = jnp.exp(top - new_top)
    weights = jnp.exp(scores - new_top[:, None]).astype(jnp.bfloat16)
    run_total = run_total * fade + jnp.sum(weights.astype(jnp.float32), axis=-1)
    run_acc = run_acc * fade[:, None] + jnp.dot(weights, values, preferred_element_type=jnp.float32)
    context = (run_acc / run_total[:, None]).astype(jnp.bfloat16)
    rows = slot // lax.axis_size("tp")
    summed = lax.psum_scatter(
        jnp.dot(context, w_out, preferred_element_type=jnp.float32).astype(jnp.bfloat16),
        "tp",
        scatter_dimension=0,
        tiled=True,
    ).astype(jnp.float32)
    index = lax.axis_index("tp") * rows + jnp.arange(rows)
    keep = index < lengths[0]
    return jnp.where(keep[:, None], summed, 0.0).astype(jnp.bfloat16)[None]


def solution(mesh):
    return jax.shard_map(
        on_device,
        mesh=mesh,
        in_specs=(
            P("req", None, "tp"),
            P("tp"),
            P(None, "tp"),
            P(None, "tp"),
            P(None, "tp"),
            P("tp", None),
            P("req", "tp"),
            P("req", "tp"),
            P("req"),
        ),
        out_specs=P("req", "tp", None),
        check_vma=False,
    )
```

profile of v0, /device:TPU:2, one launch (start us, length us, event | category | flops | bytes accessed | tf_op | source)
XLA Modules:
  0.0 325.4 jit_solution(8467891159178002061)
XLA Ops:
  6.5 0.0 copy-start
  6.5 0.0 copy-start.2
  6.5 0.0 all-gather.5.cloned.1.call-start
  6.5 0.7 all-gather.5.cloned.1.call-update
  7.3 0.0 all-gather.7.cloned.1.call-start
  7.3 0.7 all-gather.7.cloned.1.call-update
  8.0 0.0 all-gather.9.cloned.1.call-start
  8.1 0.7 all-gather.9.cloned.1.call-update
  8.7 0.0 reduce-scatter.2.cloned.1.call-start
  8.8 0.7 reshape.50
  9.5 39.7 %all-gather = bf16[16,1,256]{2,1,0:T(2,128)(2,1)S(1)} all-gather(bf16[1,1,256]{2,1,0:T(2,128)(2,1)S(1)} %reshape.50), channel_id=1, replica_groups=mesh['req'=32,'tp'=16] {'tp'}, dimensions={0}, use_global_device_ids=true | all-gather | bytes 8704 | tf_op jit(solution)/shard_map/all_gather | solution.py:23
  49.2 44.7 %all-gather.5.cloned.1.call-done = bf16[1,256,4096]{2,1,0:T(8,128)(2,1)} async-done(((bf16[1,256,256]{2,1,0:T(8,128)(2,1)}), bf16[1,256,4096]{2,1,0:T(8,128)(2,1)}) %all-gather.5.cloned.1.call-update) | async-done | bytes 2097168 | tf_op jit(solution)/shard_map/all_gather | solution.py:22
  93.9 0.0 copy-start.1
  93.9 2.2 fusion
  96.1 0.0 copy-start.3
  96.1 2.9 fusion.34
  99.0 0.0 copy-done.2
  99.0 0.0 copy-done.1
  99.0 1.0 fusion.36
  100.0 0.3 fusion.21
  100.4 0.2 fusion.38
  100.6 0.1 convert_reduce_fusion.1
  100.7 0.0 copy-done.3
  100.7 0.9 convolution_convert_fusion.1
  101.6 59.2 %all-gather.7.cloned.1.call-done = bf16[16384,128]{1,0:T(8,128)(2,1)} async-done(((bf16[512,128]{1,0:T(8,128)(2,1)}), bf16[16384,128]{1,0:T(8,128)(2,1)}) %all-gather.7.cloned.1.call-update) | async-done | bytes 4194320 | tf_op jit(solution)/shard_map/all_gather | solution.py:53
  160.7 4.6 %fusion.39 = (f32[256]{0:T(256)S(1)}, f32[256,16384]{1,0:T(8,128)S(1)}) fusion(bf16[16384,128]{1,0:T(8,128)(2,1)} %all-gather.7.cloned.1.call-done, bf16[256,64]{0,1:T(8,128)(2,1)S(1)} %get-tuple-element.13, bf16[256,64]{0,1:T(8,128)(2,1)S(1)} %get-tuple-element.14), kind=kOutput, calls=%fused_computation.57 | convolution fusion | flops 1082261248 | bytes 21038080 | tf_op jit(solution)/shard_map/sd,pd->sp/dot_general | solution.py:55
  165.4 5.4 %convert_reduce_fusion = (f32[256]{0:T(256)S(1)}, bf16[256,16384]{1,0:T(8,128)(2,1)}) fusion(f32[256,16384]{1,0:T(8,128)S(1)} %get-tuple-element.18, f32[256]{0:T(256)S(1)} %max.13), kind=kLoop, calls=%fused_computation.1 | loop fusion | flops 16776960 | bytes 25167872 | tf_op jit(solution)/shard_map/reduce_sum | solution.py:59
  170.8 56.6 %all-gather.9.cloned.1.call-done = bf16[16384,128]{1,0:T(8,128)(2,1)} async-done(((bf16[512,128]{1,0:T(8,128)(2,1)}), bf16[16384,128]{1,0:T(8,128)(2,1)}) %all-gather.9.cloned.1.call-update) | async-done | bytes 4194320 | tf_op jit(solution)/shard_map/all_gather | solution.py:54
  227.4 6.9 %fusion.40 = f32[256,128]{1,0:T(8,128)S(1)} fusion(bf16[256,16384]{1,0:T(8,128)(2,1)} %get-tuple-element.8, bf16[16384,128]{1,0:T(8,128)(2,1)} %all-gather.9.cloned.1.call-done), kind=kOutput, calls=%fused_computation.58 | convolution fusion | flops 1073741824 | bytes 12713984 | tf_op jit(solution)/shard_map/dot_general | solution.py:60
  234.3 0.0 copy-done
  234.3 2.2 convolution_convert_fusion
  236.5 0.0 reduce-scatter.2.cloned.1.call-update
  237.2 80.0 %reduce-scatter.2.cloned.1.call-done = bf16[16,4096]{1,0:T(8,128)(2,1)} async-done(((bf16[256,4096]{1,0:T(8,128)(2,1)}), bf16[16,4096]{1,0:T(8,128)(2,1)}) %reduce-scatter.2.cloned.1.call-update) | async-done | bytes 131088 | tf_op jit(solution)/shard_map/reduce_scatter | solution.py:63
  317.2 1.6 fusion.7
  (7 shorter events, 0.1 us)
Async XLA Ops:
  6.5 227.8 %copy-start = (bf16[128,4096]{1,0:T(8,128)(2,1)S(1)}, bf16[128,4096]{1,0:T(8,128)(2,1)}, u32[]{:S(2)}) copy-start(bf16[128,4096]{1,0:T(8,128)(2,1)} %param.14) | copy-start | bytes 3145732
  6.5 92.5 %copy-start.2 = (bf16[4096,128]{1,0:T(8,128)(2,1)S(1)}, bf16[4096,128]{1,0:T(8,128)(2,1)}, u32[]{:S(2)}) copy-start(bf16[4096,128]{1,0:T(8,128)(2,1)} %param.11) | copy-start | bytes 3145732
  6.5 87.3 %all-gather.5.cloned.1.call-start = ((), (), s32[]{:S(2)}) async-start(), calls=%async_computation.1 | async-start | bytes 2228224 | tf_op jit(solution)/shard_map/all_gather | solution.py:22
  7.3 153.5 %all-gather.7.cloned.1.call-start = ((), (), s32[]{:S(2)}) async-start(), calls=%async_computation.2 | async-start | bytes 4325376 | tf_op jit(solution)/shard_map/all_gather | solution.py:53
  8.0 219.4 %all-gather.9.cloned.1.call-start = ((), (), s32[]{:S(2)}) async-start(), calls=%async_computation.3 | async-start | bytes 4325376 | tf_op jit(solution)/shard_map/all_gather | solution.py:54
  8.7 308.4 %reduce-scatter.2.cloned.1.call-start = ((), (), s32[]{:S(2)}) async-start(), calls=%async_computation.4 | async-start | bytes 2228224 | tf_op jit(solution)/shard_map/reduce_scatter | solution.py:63
  93.9 5.2 %copy-start.1 = (bf16[1,256,4096]{2,1,0:T(8,128)(2,1)S(1)}, bf16[1,256,4096]{2,1,0:T(8,128)(2,1)}, u32[]{:S(2)}) copy-start(bf16[1,256,4096]{2,1,0:T(8,128)(2,1)} %all-gather.5.cloned.1.call-done) | copy-start | bytes 6291460
  96.1 4.6 %copy-start.3 = (bf16[4096,128]{1,0:T(8,128)(2,1)S(1)}, bf16[4096,128]{1,0:T(8,128)(2,1)}, u32[]{:S(2)}) copy-start(bf16[4096,128]{1,0:T(8,128)(2,1)} %param.13) | copy-start | bytes 3145732
Sparse Core Ops, SparseCore 0:
  9.3 84.4 all-gather.4
  97.0 63.7 all-gather.6
  163.9 63.4 all-gather.8
  236.7 80.4 reduce-scatter.1
where the time goes:
time: 326 us; the launch traced here: 325 us
  waiting for transfers between devices  243 us (75%)
  blocking collectives  39.7 us (12%)
  matrix products  18.7 us (6%)
  between operations  13.9 us (4%)
  other arithmetic  9.72 us (3%)
    reduce_scatter x1, waiting for transfers between devices, on_device(): lax.psum_scatter(jnp.dot(context, w_out, preferred_element_type=jnp.float...  80 us
    all_gather x1, waiting for transfers between devices, on_device(): keys = lax.all_gather(prefix_keys, 'req', axis=0, tiled=True)  59.2 us
    all_gather x1, waiting for transfers between devices, on_device(): values = lax.all_gather(prefix_values, 'req', axis=0, tiled=True)  56.6 us
    all_gather x1, waiting for transfers between devices, on_device(): lax.all_gather(hidden, 'tp', axis=2, tiled=True)  44.7 us
    all_gather x1, blocking collectives, on_device(): lax.all_gather(norm_gain, 'tp', axis=0, tiled=True)  39.7 us
    dot_general x1, matrix products, on_device(): jnp.dot(weights, values, preferred_element_type=jnp.float32)  6.9 us
  transfers between devices with their start and end apart: 4, of which 4 were waited for; matrix products, arithmetic and copies ran while one was open for 6% of the time, Pallas kernels for 0%

commit v1 on v0

--- a/solution.py
+++ b/solution.py
@@ -2,6 +2,11 @@
 import jax.numpy as jnp
 from jax import lax
 from jax.sharding import PartitionSpec as P
+
+
+def swapped_in(x, axis, dim):
+    sent = jnp.stack([x] * lax.axis_size(axis))
+    return jnp.concatenate(lax.all_to_all(sent, axis, 0, 0), axis=dim)
 
 
 def rotate(values, angles):
@@ -51,7 +56,7 @@
     run_total = total
     run_acc = acc
     keys = lax.all_gather(prefix_keys, "req", axis=0, tiled=True)
-    values = lax.all_gather(prefix_values, "req", axis=0, tiled=True)
+    values = swapped_in(prefix_values, "req", 0)
     scores = jnp.einsum("sd,pd->sp", query, keys, preferred_element_type=jnp.float32) * scale
     new_top = jnp.maximum(top, jnp.max(scores, axis=-1))
     fade = jnp.exp(top - new_top)

time: 326 us -> 340 us (1.043)
  the two profiles are of different devices: /device:TPU:2 before, /device:TPU:4 now
where the time goes in v1:
time: 340 us
  blocking collectives  165 us (49%)
  waiting for transfers between devices  118 us (35%)
  matrix products  18.5 us (5%)
  between operations  13.9 us (4%)
  starting transfers between devices  10.5 us (3%)
  other arithmetic  9.71 us (3%)
  local copies, waits for them, and re-layouts  3.82 us (1%)
    all_gather x1, blocking collectives, on_device(): lax.all_gather(norm_gain, 'tp', axis=0, tiled=True)  165 us
    reduce_scatter x1, waiting for transfers between devices, on_device(): lax.psum_scatter(jnp.dot(context, w_out, preferred_element_type=jnp.float...  80 us
    all_gather x1, waiting for transfers between devices, on_device(): keys = lax.all_gather(prefix_keys, 'req', axis=0, tiled=True)  36.9 us
    all_to_all x1, starting transfers between devices, swapped_in(): return jnp.concatenate(lax.all_to_all(sent, axis, 0, 0), axis=dim)  10.4 us
    dot_general x1, matrix products, on_device(): jnp.dot(weights, values, preferred_element_type=jnp.float32)  6.91 us
  transfers between devices with their start and end apart: 4, of which 2 were waited for; matrix products, arithmetic and copies ran while one was open for 6% of the time, Pallas kernels for 0%

profile of v1, /device:TPU:4, one launch (start us, length us, event | category | flops | bytes accessed | tf_op | source)
XLA Modules:
  0.0 339.5 jit_solution(10793415863884733509)
XLA Ops:
  6.5 0.0 copy-start
  6.5 0.0 all-gather.4.cloned.1.call-start
  6.5 0.7 all-gather.4.cloned.1.call-update
  7.3 0.0 all-gather.6.cloned.1.call-start
  7.3 0.7 all-gather.6.cloned.1.call-update
  8.0 3.8 %stack.2 = bf16[32,512,128]{2,1,0:T(8,128)(2,1)} broadcast(bf16[512,128]{1,0:T(8,128)(2,1)} %param.16), dimensions={1,2} | broadcast | bytes 4325376 | tf_op jit(solution)/shard_map/stack | solution.py:8
  11.8 0.0 copy-start.5
  11.8 0.0 copy-start.2
  11.8 10.4 %all-to-all-start = ((bf16[32,512,128]{2,1,0:T(8,128)(2,1)}), bf16[32,512,128]{2,1,0:T(8,128)(2,1)}, u32[]{:S(2)}, u32[]{:S(2)}) async-start(bf16[32,512,128]{2,1,0:T(8,128)(2,1)} %stack.2), calls=%async_computation | async-start | bytes 8388608 | tf_op jit(solution)/shard_map/all_to_all | solution.py:9
  22.2 0.0 copy-start.3
  22.3 0.0 reduce-scatter.2.cloned.1.call-start
  22.3 0.0 copy-done.5
  22.3 164.8 %all-gather = bf16[16,1,256]{2,1,0:T(2,128)(2,1)S(1)} all-gather(bf16[1,1,256]{2,1,0:T(2,128)(2,1)S(1)} %reshape.56), channel_id=1, replica_groups=mesh['req'=32,'tp'=16] {'tp'}, dimensions={0}, use_global_device_ids=true | all-gather | bytes 8704 | tf_op jit(solution)/shard_map/all_gather | solution.py:28
  187.1 0.0 all-gather.4.cloned.1.call-done
  187.2 0.0 copy-start.1
  187.2 2.2 fusion
  189.4 0.0 copy-done.2
  189.4 0.0 copy-start.4
  189.5 2.6 fusion.34
  192.1 0.0 copy-done.3
  192.1 0.0 copy-done.1
  192.1 1.0 fusion.36
  193.1 0.3 fusion.21
  193.4 0.2 fusion.38
  193.7 0.1 convert_reduce_fusion.1
  193.8 0.0 copy-done.4
  193.8 0.9 convolution_convert_fusion.1
  194.6 36.9 %all-gather.6.cloned.1.call-done = bf16[16384,128]{1,0:T(8,128)(2,1)} async-done(((bf16[512,128]{1,0:T(8,128)(2,1)}), bf16[16384,128]{1,0:T(8,128)(2,1)}) %all-gather.6.cloned.1.call-update) | async-done | bytes 4194320 | tf_op jit(solution)/shard_map/all_gather | solution.py:58
  231.5 4.6 %fusion.39 = (f32[256]{0:T(256)S(1)}, f32[256,16384]{1,0:T(8,128)S(1)}) fusion(bf16[16384,128]{1,0:T(8,128)(2,1)} %all-gather.6.cloned.1.call-done, bf16[256,64]{0,1:T(8,128)(2,1)S(1)} %get-tuple-element.13, bf16[256,64]{0,1:T(8,128)(2,1)S(1)} %get-tuple-element.14), kind=kOutput, calls=%fused_computation.57 | convolution fusion | flops 1082261248 | bytes 21038080 | tf_op jit(solution)/shard_map/sd,pd->sp/dot_general | solution.py:60
  236.2 5.3 %convert_reduce_fusion = (f32[256]{0:T(256)S(1)}, bf16[256,16384]{1,0:T(8,128)(2,1)}) fusion(f32[256,16384]{1,0:T(8,128)S(1)} %get-tuple-element.18, f32[256]{0:T(256)S(1)} %max.13), kind=kLoop, calls=%fused_computation.1 | loop fusion | flops 16776960 | bytes 25167872 | tf_op jit(solution)/shard_map/reduce_sum | solution.py:64
  241.5 0.0 all-to-all-done
  241.5 6.9 %fusion.40 = f32[256,128]{1,0:T(8,128)S(1)} fusion(bf16[256,16384]{1,0:T(8,128)(2,1)} %get-tuple-element.8, bf16[16384,128]{1,0:T(8,128)(2,1)} %bitcast.4), kind=kOutput, calls=%fused_computation.58 | convolution fusion | flops 1073741824 | bytes 12713984 | tf_op jit(solution)/shard_map/dot_general | solution.py:65
  248.4 0.0 copy-done
  248.4 2.2 convolution_convert_fusion
  250.6 0.0 reduce-scatter.2.cloned.1.call-update
  251.3 80.0 %reduce-scatter.2.cloned.1.call-done = bf16[16,4096]{1,0:T(8,128)(2,1)} async-done(((bf16[256,4096]{1,0:T(8,128)(2,1)}), bf16[16,4096]{1,0:T(8,128)(2,1)}) %reduce-scatter.2.cloned.1.call-update) | async-done | bytes 131088 | tf_op jit(solution)/shard_map/reduce_scatter | solution.py:68
  331.3 1.6 fusion.7
  (8 shorter events, 0.1 us)
Async XLA Ops:
  6.5 241.9 %copy-start = (bf16[128,4096]{1,0:T(8,128)(2,1)S(1)}, bf16[128,4096]{1,0:T(8,128)(2,1)}, u32[]{:S(2)}) copy-start(bf16[128,4096]{1,0:T(8,128)(2,1)} %param.14) | copy-start | bytes 3145732
  6.5 180.6 %all-gather.4.cloned.1.call-start = ((), (), s32[]{:S(2)}) async-start(), calls=%async_computation.2 | async-start | bytes 2228224 | tf_op jit(solution)/shard_map/all_gather | solution.py:27
  7.3 224.2 %all-gather.6.cloned.1.call-start = ((), (), s32[]{:S(2)}) async-start(), calls=%async_computation.3 | async-start | bytes 4325376 | tf_op jit(solution)/shard_map/all_gather | solution.py:58
  11.8 10.5 %copy-start.5 = (bf16[256]{0:T(256)(128)(2,1)S(1)}, bf16[256]{0:T(256)(128)(2,1)}, u32[]{:S(2)}) copy-start(bf16[256]{0:T(256)(128)(2,1)} %param.10) | copy-start | bytes 1540
  11.8 177.6 %copy-start.2 = (bf16[4096,128]{1,0:T(8,128)(2,1)S(1)}, bf16[4096,128]{1,0:T(8,128)(2,1)}, u32[]{:S(2)}) copy-start(bf16[4096,128]{1,0:T(8,128)(2,1)} %param.12) | copy-start | bytes 3145732
  11.8 229.7 %all-to-all-start = ((bf16[32,512,128]{2,1,0:T(8,128)(2,1)}), bf16[32,512,128]{2,1,0:T(8,128)(2,1)}, u32[]{:S(2)}, u32[]{:S(2)}) async-start(bf16[32,512,128]{2,1,0:T(8,128)(2,1)} %stack.2), calls=%async_computation | async-start | bytes 8388608 | tf_op jit(solution)/shard_map/all_to_all | solution.py:9
  22.2 169.9 %copy-start.3 = (bf16[4096,128]{1,0:T(8,128)(2,1)S(1)}, bf16[4096,128]{1,0:T(8,128)(2,1)}, u32[]{:S(2)}) copy-start(bf16[4096,128]{1,0:T(8,128)(2,1)} %param.11) | copy-start | bytes 3145732
  22.3 309.1 %reduce-scatter.2.cloned.1.call-start = ((), (), s32[]{:S(2)}) async-start(), calls=%async_computation.4 | async-start | bytes 2228224 | tf_op jit(solution)/shard_map/reduce_scatter | solution.py:68
  187.2 4.9 %copy-start.1 = (bf16[1,256,4096]{2,1,0:T(8,128)(2,1)S(1)}, bf16[1,256,4096]{2,1,0:T(8,128)(2,1)}, u32[]{:S(2)}) copy-start(bf16[1,256,4096]{2,1,0:T(8,128)(2,1)} %all-gather.4.cloned.1.call-done) | copy-start | bytes 6291460
  189.4 4.3 %copy-start.4 = (bf16[4096,128]{1,0:T(8,128)(2,1)S(1)}, bf16[4096,128]{1,0:T(8,128)(2,1)}, u32[]{:S(2)}) copy-start(bf16[4096,128]{1,0:T(8,128)(2,1)} %param.13) | copy-start | bytes 3145732
Sparse Core Ops, SparseCore 0:
  9.3 154.1 all-gather.3
  166.6 64.8 all-gather.5
  250.8 80.5 reduce-scatter.1
